TPU v7x, 512 devices: a whole 4x8x8 slice. The times are simulated.
512 devices in a mesh: head: 8 (over y_hi, x), blk: 64 (over y_lo, z, core).
Axes of the slice: x: 4, y: 8 (y_hi: 2, y_lo: 4; y = y_hi * 4 + y_lo), z: 8, core: 2. Of those that a mesh axis runs over, the one named last changes fastest.
Arguments:
- query_rows: bfloat16 [8192, 1536], P(('head', 'blk')), may hold values from -400 to 400
- key_rows: bfloat16 [8192, 1536], P(('head', 'blk')), may hold values from -400 to 400
- value_rows: bfloat16 [8192, 1536], P(('head', 'blk')), may hold values from -6 to 6
- residual: bfloat16 [8192, 1536], P(('head', 'blk')), may hold values from -6 to 6
- out_weight: bfloat16 [1536, 1536], P('head'), may hold values from -0.15625 to 0.15625
- attention_gate: float32 [1536], replicated, may hold values from 0.5 to 1.5
- norm_shift: float32 [1536], replicated, may hold values from -1 to 1
- norm_scale: float32 [1536], replicated, may hold values from -0.5 to 0.5
- expert_gate: float32 [1536], replicated, may hold values from 0.5 to 1.5
- expert_up: bfloat16 [64, 1536, 4096], P('blk', None, 'head'), may hold values from -0.15625 to 0.15625
- expert_down: bfloat16 [64, 4096, 1536], P('blk', 'head'), may hold values from -0.09375 to 0.09375
- routing: int32 [8192, 2], P(('head', 'blk')), may hold values from 0 to 63, as said below
- combine_weight: float32 [8192, 2], P(('head', 'blk')), may hold values from 0.2 to 1
Outputs:
- mixed: bfloat16 [8192, 1536], P(('head', 'blk'))
Inputs may be any that keep to these rules, and one draw needn't show every extreme that they name: `routing`: the two choices of a token differ. Within the 16 tokens of one device every expert is named at most 2 times, and one expert, the same for every device, is named exactly 2 times by every device.
All inputs are finite; a program needn't handle non-finite values.
Results may differ from a plain program's by a relative error of at most 0.011.
Values may be sent and summed in bfloat16 or wider, within the bound.
No kernel may reach another device: no remote copies, remote signals or barrier semaphores. Data moves between devices by JAX's collectives and lax.ppermute only.
A program may use at most 64 MiB of HBM per device.

v0:
```python
import math

import jax
import jax.numpy as jnp
from jax import lax
from jax.experimental import pallas as pl
from jax.experimental.pallas import tpu as pltpu
from jax.sharding import Mesh
from jax.sharding import PartitionSpec as P

HD = 64
TOPK = 2
SLOTS = 2
LANES = 128
AXES = ("yh", "x", "yl", "z", "c")
HEAD = ("yh", "x")
BLK = ("yl", "z", "c")
PLANE = ("yl", "z")
BF16 = jnp.bfloat16
F32 = jnp.float32
RATE = math.log2(math.e) / math.sqrt(HD)


def exchange(array, axis):
    return lax.all_to_all(array, axis, 0, 0, tiled=True)


def gathered(array, axis):
    copies = jnp.broadcast_to(array[None], (lax.axis_size(axis), *array.shape))
    return exchange(copies, axis)


def partner(array, axis):
    return lax.ppermute(array, axis, [(0, 1), (1, 0)])


def shifted(array, by, axis="x"):
    n = lax.axis_size(axis)
    return lax.ppermute(array, axis, [(i, (i + by) % n) for i in range(n)])


def iota(shape, dim):
    return lax.broadcasted_iota(jnp.int32, shape, dim)


def dot(a, b, dims=((1,), (0,))):
    return lax.dot_general(a, b, (dims, ((), ())), preferred_element_type=F32)


def pieces(values):
    out = []
    for _ in range(3):
        piece = values.astype(BF16).astype(F32)
        out.append(piece)
        values = values - piece
    return out


def local(body, outs, *args, smem=(), **kw):
    specs = [
        pl.BlockSpec(memory_space=pltpu.SMEM if i in smem else pltpu.VMEM)
        for i in range(len(args))
    ]
    return pl.pallas_call(
        body,
        out_shape=outs,
        in_specs=specs,
        out_specs=jax.tree.map(lambda _: pl.BlockSpec(memory_space=pltpu.VMEM), outs),
        **kw,
    )(*args)


def shape(dims, kind=BF16):
    return jax.ShapeDtypeStruct(dims, kind)


def prepare(q_ref, k_ref, v_ref, route_ref, weight_ref, out_ref):
    groups, tok, _ = out_ref.shape
    cols = q_ref.shape[1] // groups
    weight = weight_ref[...]
    lines = [route_ref[k : k + 1, :].astype(F32) for k in range(TOPK)]
    for piece in pieces(weight):
        lines += [piece[k : k + 1, :] for k in range(TOPK)]
    row = iota((16, tok), 0)
    table = jnp.zeros((16, tok), F32)
    for i, line in enumerate(lines):
        table = jnp.where(row == i, line, table)
    pick = (iota((16, HD), 0) == iota((16, HD), 1)).astype(BF16)
    header = dot(table.astype(BF16), pick, ((0,), (0,))).astype(BF16)
    for g in range(groups):
        span = slice(g * cols, (g + 1) * cols)
        out_ref[g] = jnp.concatenate(
            [q_ref[:, span], header, k_ref[:, span], v_ref[:, span]], axis=1
        )


def attend(q_ref, near_ref, far_ref, out_ref):
    rows, cols = q_ref.shape[0], q_ref.shape[1] - HD
    heads = cols // HD
    q = q_ref[:, :cols]
    near_k, far_k = near_ref[:, :cols], far_ref[:, :cols]
    near_v, far_v = near_ref[:, LANES:], far_ref[:, LANES:]
    q_head = iota((rows, cols), 1) // HD
    lane = iota((rows, cols + HD), 1)
    out = jnp.zeros((rows, cols + HD), F32)
    for j in range(heads):
        q_j = jnp.where(q_head == j, q, jnp.zeros_like(q))
        near = dot(q_j, near_k, ((1,), (1,)))
        far = dot(q_j, far_k, ((1,), (1,)))
        peak = jnp.maximum(
            jnp.max(near, axis=1, keepdims=True), jnp.max(far, axis=1, keepdims=True)
        )
        near = jnp.exp2((near - peak) * RATE)
        far = jnp.exp2((far - peak) * RATE)
        total = jnp.sum(near, axis=1, keepdims=True) + jnp.sum(far, axis=1, keepdims=True)
        accum = dot(near.astype(BF16), near_v) + dot(far.astype(BF16), far_v)
        out = jnp.where(lane // HD == j + 1, accum * (1.0 / total), out)
        for i, piece in enumerate(pieces(peak) + pieces(total)):
            out = jnp.where(lane == 6 * j + i, piece, out)
    out_ref[...] = out.astype(BF16)


def project(parts_ref, weight_ref, out_ref):
    count, rows, wide = parts_ref.shape
    n_x, pair_rows, _ = out_ref.shape
    tok = pair_rows // 2
    stats = parts_ref[:, :, :LANES].reshape(count * rows, LANES)
    src = iota((LANES, wide), 0)
    head = jnp.maximum(iota((LANES, wide), 1) // HD - 1, 0)
    at = src - 6 * head
    peak = dot(stats, ((at >= 0) & (at < 3)).astype(BF16)).reshape(count, rows, wide)
    total = dot(stats, ((at >= 3) & (at < 6)).astype(BF16)).reshape(count, rows, wide)
    top = jnp.max(peak, axis=0)
    share = total * jnp.exp2((peak - top[None]) * RATE)
    numer = jnp.sum(share * parts_ref[...].astype(F32), axis=0)
    attended = (numer / jnp.sum(share, axis=0))[:, HD:].astype(BF16)
    projected = dot(attended, weight_ref[...]).astype(BF16)
    for side in range(2):
        for x in range(n_x):
            start = (side * n_x + x) * tok
            out_ref[x, side * tok : (side + 1) * tok, :] = projected[start : start + tok]


def normalize(
    where_ref, sum_ref, got_ref, residual_ref, shift_ref, factor_ref, own_ref, middle_ref, out_ref
):
    tok, width = residual_ref.shape
    own, x, n_x = where_ref[0], where_ref[1], own_ref.shape[0] // (2 * tok)
    residual = residual_ref[...].astype(F32)
    for side in range(2):
        span = slice(side * tok, (side + 1) * tok)
        added = jnp.where(own == side, residual, 0.0)
        middle = sum_ref[span, :] + got_ref[span, :].astype(F32) + added

        @pl.when(own == side)
        def _():
            middle_ref[...] = middle

        average = jnp.mean(middle, axis=1, keepdims=True)
        centered = middle - average
        variance = jnp.mean(centered * centered, axis=1, keepdims=True)
        scaled = centered * lax.rsqrt(variance + 1e-06) * factor_ref[...]
        out_ref[span, :width] = (scaled + shift_ref[...]).astype(BF16)
        start = pl.multiple_of((side * n_x + x) * tok, tok)
        out_ref[span, width:] = own_ref[pl.ds(start, tok), LANES : 2 * LANES]


def places(near_ref, far_ref, c, width, across):
    pair = near_ref.shape[0]
    tok = pair // 2
    count = 2 * pair
    headers = jnp.concatenate([near_ref[:, width:], far_ref[:, width:]], axis=0)
    take = (iota((8, LANES), 1) == iota((8, LANES), 0) + HD).astype(BF16)
    lines = dot(take, headers, ((1,), (1,)))
    headers = headers.astype(F32)
    lane = iota((count, LANES), 1)

    def column(i):
        return jnp.sum(jnp.where(lane == HD + i, headers, 0.0), axis=1, keepdims=True)

    line = [lines[k : k + 1, :] for k in range(TOPK)]
    col = [column(k) for k in range(TOPK)]
    named, others, axis = (line, col, 0) if across else (col, line, 1)
    this, other = iota((count, count), 1 - axis), iota((count, count), axis)
    before = (other < this) & (this // tok == other // tok)
    group = iota((1, count), 1) // tok if across else iota((count, 1), 0) // tok
    out = []
    for k in range(TOPK):
        same = sum((other_k == named[k]).astype(F32) for other_k in others)
        slot = jnp.sum(jnp.where(before, same, 0.0), axis=axis, keepdims=True).astype(jnp.int32)
        expert = named[k].astype(jnp.int32)
        place = (expert // 2) * (4 * SLOTS) + group * SLOTS + slot
        out.append(jnp.where(expert % 2 == c, place, -1))
    return out, column


def dispatch(where_ref, near_ref, far_ref, out_ref):
    rows, width = out_ref.shape
    pair = near_ref.shape[0]
    chosen, _ = places(near_ref, far_ref, where_ref[2], width, True)
    target = iota((rows, 2 * pair), 0)
    onehot = sum((target == place).astype(F32) for place in chosen).astype(BF16)
    out_ref[...] = (
        dot(onehot[:, :pair], near_ref[:, :width]) + dot(onehot[:, pair:], far_ref[:, :width])
    ).astype(BF16)


def run_expert(rows_ref, *refs):
    *weights, out_ref, up_buf, down_buf, sem = refs
    count = len(weights) // 2
    ups, downs = weights[:count], weights[count:]
    copies = []
    for i in range(count):
        copies.append(
            (
                pltpu.make_async_copy(ups[i], up_buf.at[i], sem.at[0, i]),
                pltpu.make_async_copy(downs[i], down_buf.at[i], sem.at[1, i]),
            )
        )
        for copy in copies[-1]:
            copy.start()
    rows = rows_ref[...]
    total = jnp.zeros(out_ref.shape, F32)
    for i in range(count):
        copies[i][0].wait()
        hidden = jax.nn.gelu(dot(rows, up_buf[i]), approximate=True).astype(BF16)
        copies[i][1].wait()
        total = total + dot(hidden, down_buf[i])
    out_ref[...] = total.astype(BF16)


def mix(where_ref, near_ref, far_ref, rows_ref, kept_ref, given_ref):
    rows, width = rows_ref.shape
    pair = near_ref.shape[0]
    chosen, column = places(near_ref, far_ref, where_ref[2], width, False)
    source = iota((2 * pair, rows), 1)
    pick = jnp.zeros((2 * pair, rows), F32)
    for k, place in enumerate(chosen):
        weight = sum(column(TOPK * (1 + i) + k) for i in range(3))
        pick = pick + jnp.where(source == place, weight, 0.0)
    high, low, _ = pieces(pick)
    returned = rows_ref[...]
    mixed = dot(high.astype(BF16), returned) + dot(low.astype(BF16), returned)
    kept_ref[...] = mixed[:pair]
    given_ref[...] = mixed[pair:].astype(BF16)


def layer(
    query_rows,
    key_rows,
    value_rows,
    residual,
    out_weight,
    attention_gate,
    norm_shift,
    norm_scale,
    expert_gate,
    expert_up,
    expert_down,
    routing,
    combine_weight,
):
    tok, width = query_rows.shape
    n_head = lax.axis_size(HEAD)
    n_x = lax.axis_size("x")
    n_z = lax.axis_size("z")
    n_plane = lax.axis_size(PLANE)
    cols = width // n_head
    rows = n_head * tok
    where = jnp.stack([lax.axis_index(a) for a in ("yh", "x", "c")]).astype(jnp.int32)
    factor = (1.0 + norm_scale).reshape(1, width)
    gate, shift = (a.reshape(1, width) for a in (attention_gate, norm_shift))

    own = local(
        prepare,
        shape((n_head, tok, 3 * cols + HD)),
        query_rows,
        key_rows,
        value_rows,
        routing.T,
        combine_weight.T,
    )
    own = exchange(own, HEAD).reshape(rows, 3 * cols + HD)

    up, down = expert_up[0], expert_down[0]
    up_left, up_right = shifted(up, 1), shifted(up, -1)
    down_left, down_right = shifted(down, 1), shifted(down, -1)
    up_far, down_far = shifted(up_left, 1), shifted(down_right, -1)
    near = own[:, cols + HD :]
    near = jnp.concatenate([near] + [shifted(near, turn, "yl") for turn in (1, 2, 3)], axis=0)
    far = partner(near, "c")
    queries = gathered(own[:, : cols + HD], "z").reshape(-1, cols + HD)

    q_block = 256
    whole = pl.BlockSpec(near.shape, lambda i: (0, 0))
    packed = pl.pallas_call(
        attend,
        grid=(queries.shape[0] // q_block,),
        in_specs=[pl.BlockSpec((q_block, cols + HD), lambda i: (i, 0)), whole, whole],
        out_specs=pl.BlockSpec((q_block, cols + HD), lambda i: (i, 0)),
        out_shape=shape((queries.shape[0], cols + HD)),
        name="attend",
    )(queries, near, far)
    packed = exchange(packed.reshape(n_z, rows, cols + HD), "z")

    partial = local(project, shape((n_x, 2 * tok, width)), packed, out_weight)
    parts = exchange(partial, "x")
    gated = jnp.sum(parts.astype(F32), axis=0) * gate
    first = where[0] == 0
    ours = jnp.where(first, gated[:tok], gated[tok:]) + residual.astype(F32)
    message = jnp.concatenate(
        [jnp.where(first, ours, gated[:tok]), jnp.where(first, gated[tok:], ours)], axis=0
    ).astype(BF16)
    middle, near = local(
        normalize,
        (shape((tok, width), F32), shape((2 * tok, width + LANES))),
        where,
        gated,
        partner(message, "yh"),
        residual,
        shift,
        factor,
        own,
        smem=(0,),
    )
    far = partner(near, "c")

    buffer_rows = n_plane * 4 * SLOTS
    sent = local(dispatch, shape((buffer_rows, width)), where, near, far, smem=(0,))
    arrived = exchange(sent.reshape(n_plane, -1, width), PLANE).reshape(buffer_rows, width)
    ups, downs = (up, up_left, up_right, up_far), (down, down_left, down_right, down_far)
    in_place = pl.BlockSpec(memory_space=pl.ANY)
    output = pl.pallas_call(
        run_expert,
        in_specs=[pl.BlockSpec(memory_space=pltpu.VMEM)] + [in_place] * (2 * n_x),
        out_specs=pl.BlockSpec(memory_space=pltpu.VMEM),
        out_shape=shape((buffer_rows, width)),
        scratch_shapes=[
            pltpu.VMEM((n_x, *up.shape), BF16),
            pltpu.VMEM((n_x, *down.shape), BF16),
            pltpu.SemaphoreType.DMA((2, n_x)),
        ],
        name="run_expert",
    )(arrived, *ups, *downs)
    returned = exchange(output.reshape(n_plane, -1, width), PLANE).reshape(buffer_rows, width)

    kept, given = local(
        mix,
        (shape((2 * tok, width), F32), shape((2 * tok, width))),
        where,
        near,
        far,
        returned,
        smem=(0,),
    )
    both = kept + partner(given, "c").astype(F32)
    low, high = both[:tok], both[tok:]
    given = jnp.where(first, high, low).astype(BF16)
    mixture = jnp.where(first, low, high) + partner(given, "yh").astype(F32)
    return (middle + expert_gate * mixture).astype(BF16)


def solution(mesh):
    split = Mesh(mesh.devices.reshape(2, 4, 4, 8, 2), AXES)
    everywhere = P(AXES, None)
    placed = (
        everywhere,
        everywhere,
        everywhere,
        everywhere,
        P(HEAD, None),
        P(),
        P(),
        P(),
        P(),
        P(BLK, None, HEAD),
        P(BLK, HEAD, None),
        everywhere,
        everywhere,
    )
    return jax.shard_map(layer, mesh=split, in_specs=placed, out_specs=everywhere, check_vma=False)
```

profile of v0, /device:TPU:1, one launch (start us, length us, event | category | flops | bytes accessed | tf_op | source)
XLA Modules:
  0.0 255.0 jit_solution(994682191060419206)
XLA Ops:
  0.0 1.8 shard_map.127
  1.8 19.7 %all_to_all.30 = bf16[8,16,640]{2,1,0:T(8,128)(2,1)S(1)} all-to-all(bf16[8,16,640]{2,1,0:T(8,128)(2,1)} %shard_map.127), channel_id=1, replica_groups=mesh['yh'=2,'x'=4,'yl'=4,'z'=8,'c'=2] {'yh','x'}, dimensions={0} | all-to-all | bytes 327680 | tf_op jit(solution)/shard_map/all_to_all | solution.py:25
  21.5 0.8 broadcast_in_dim.2
  22.3 10.0 %all-to-all-start.1 = ((bf16[8,128,256]{2,1,0:T(8,128)(2,1)}), bf16[8,128,256]{2,1,0:T(8,128)(2,1)S(1)}, u32[]{:S(2)}, u32[]{:S(2)}) async-start(bf16[8,128,256]{2,1,0:T(8,128)(2,1)} %broadcast_in_dim.2), calls=%async_computation.1 | async-start | bytes 1048576 | tf_op jit(solution)/shard_map/all_to_all | solution.py:25
  32.4 2.5 collective-permute-start.2
  34.9 4.4 %collective-permute-start.1 = (bf16[128,384]{1,0:T(8,128)(2,1)S(1)}, bf16[128,384]{1,0:T(8,128)(2,1)S(1)}, u32[]{:S(2)}, u32[]{:S(2)}) collective-permute-start(bf16[128,384]{1,0:T(8,128)(2,1)S(1)} %slice.27), channel_id=1, source_target_pairs={{0,32},{16,48},{32,0},{48,16},{1,33},{17,49},{33,1},{49,17},{2,34}... | collective-permute-start | bytes 294920 | tf_op jit(solution)/shard_map/ppermute | solution.py:39
  39.3 1.9 collective-permute-start
  41.3 0.0 collective-permute-done.2
  41.3 2.0 collective-permute-done.1
  43.3 3.3 %collective-permute-done = bf16[128,384]{1,0:T(8,128)(2,1)S(1)} collective-permute-done((bf16[128,384]{1,0:T(8,128)(2,1)S(1)}, bf16[128,384]{1,0:T(8,128)(2,1)S(1)}, u32[]{:S(2)}, u32[]{:S(2)}) %collective-permute-start) | collective-permute-done | bytes 98336 | tf_op jit(solution)/shard_map/ppermute | solution.py:39
  46.6 0.0 copy-start.4
  46.7 5.4 %collective-permute-start.3 = (bf16[512,384]{1,0:T(8,128)(2,1)S(1)}, bf16[512,384]{1,0:T(8,128)(2,1)S(1)}, u32[]{:S(2)}, u32[]{:S(2)}) collective-permute-start(bf16[512,384]{1,0:T(8,128)(2,1)S(1)} %pad_maximum_fusion.near_ref), channel_id=1, source_target_pairs={{0,1},{1,0},{2,3},{3,2},{4,5},{5,4},{6,7},{7,6},{8,9},{9,8},{10,11... | collective-permute-start | bytes 1179656 | tf_op jit(solution)/shard_map/ppermute | solution.py:34
  52.1 1.3 collective-permute-done.3.far_ref
  53.4 0.0 all-to-all-done.1
  53.4 0.0 copy-done.4
  53.4 0.8 copy-done.7
  54.2 0.2 copy-done.1
  54.4 8.6 %attend.1 = bf16[1024,256]{1,0:T(8,128)(2,1)} custom-call(bf16[1024,256]{1,0:T(8,128)(2,1)} %bitcast.18, bf16[512,384]{1,0:T(8,128)(2,1)} %copy-done.4, bf16[512,384]{1,0:T(8,128)(2,1)} %copy-done.7), custom_call_target="tpu_custom_call" | custom-call | tf_op jit(solution)/shard_map/attend/pallas_call | solution.py:296
  63.0 0.0 copy-done.5
  63.0 0.0 copy-start.14
  63.1 23.9 %all_to_all.31.parts_ref = bf16[8,128,256]{2,1,0:T(8,128)(2,1)} all-to-all(bf16[8,128,256]{2,1,0:T(8,128)(2,1)} %bitcast.19), channel_id=1, replica_groups=mesh['yh'=2,'x'=4,'yl'=4,'z'=8,'c'=2] {'z'}, dimensions={0} | all-to-all | bytes 1048576 | tf_op jit(solution)/shard_map/all_to_all | solution.py:25
  87.0 3.0 %shard_map.128 = bf16[4,32,1536]{2,1,0:T(8,128)(2,1)} custom-call(bf16[8,128,256]{2,1,0:T(8,128)(2,1)} %all_to_all.31.parts_ref, bf16[192,1536]{1,0:T(8,128)(2,1)} %weight_ref.1), custom_call_target="tpu_custom_call" | custom-call | tf_op jit(solution)/shard_map/pallas_call | solution.py:64
  89.9 3.5 %all-to-all-start.3 = ((bf16[4,32,1536]{2,1,0:T(8,128)(2,1)}), bf16[4,32,1536]{2,1,0:T(8,128)(2,1)S(1)}, u32[]{:S(2)}, u32[]{:S(2)}) async-start(bf16[4,32,1536]{2,1,0:T(8,128)(2,1)} %shard_map.128), calls=%async_computation.3 | async-start | bytes 786432 | tf_op jit(solution)/shard_map/all_to_all | solution.py:25
  93.4 0.0 copy-done.3
  93.4 3.3 %collective-permute-start.6 = (bf16[1536,512]{1,0:T(8,128)(2,1)S(1)}, bf16[1536,512]{1,0:T(8,128)(2,1)}, u32[]{:S(2)}, u32[]{:S(2)}) collective-permute-start(bf16[1536,512]{1,0:T(8,128)(2,1)S(1)} %bitcast.21), channel_id=1, source_target_pairs={{0,64},{64,128},{128,192},{192,0},{1,65},{65,129},{129,193},{193,1... | collective-permute-start | bytes 4718600 | tf_op jit(solution)/shard_map/ppermute | solution.py:39
  96.7 3.2 %collective-permute-start.10 = (bf16[512,1536]{1,0:T(8,128)(2,1)}, bf16[512,1536]{1,0:T(8,128)(2,1)}, u32[]{:S(2)}, u32[]{:S(2)}) collective-permute-start(bf16[512,1536]{1,0:T(8,128)(2,1)} %bitcast.11.refs_4_), channel_id=1, source_target_pairs={{0,192},{64,0},{128,64},{192,128},{1,193},{65,1},{129,65},{193,129... | collective-permute-start | bytes 4718600 | tf_op jit(solution)/shard_map/ppermute | solution.py:39
  99.9 0.6 reshape.34.shift_ref
  100.5 0.0 copy-done.14
  100.5 0.6 reshape.35.factor_ref
  101.1 0.0 all-to-all-done.3
  101.1 0.1 convert_reduce_fusion
  101.3 2.2 collective-permute-start.4
  103.5 0.7 pad_add_fusion.where_ref
  104.1 6.5 %collective-permute-done.4.got_ref = bf16[32,1536]{1,0:T(8,128)(2,1)S(1)} collective-permute-done((bf16[32,1536]{1,0:T(8,128)(2,1)S(1)}, bf16[32,1536]{1,0:T(8,128)(2,1)S(1)}, u32[]{:S(2)}, u32[]{:S(2)}) %collective-permute-start.4) | collective-permute-done | bytes 98336 | tf_op jit(solution)/shard_map/ppermute | solution.py:34
  110.7 0.0 copy-done.2
  110.7 0.6 copy-done.9
  111.3 2.2 shard_map.129
  113.5 6.0 %collective-permute-start.5 = (bf16[32,1664]{1,0:T(8,128)(2,1)}, bf16[32,1664]{1,0:T(8,128)(2,1)S(1)}, u32[]{:S(2)}, u32[]{:S(2)}) collective-permute-start(bf16[32,1664]{1,0:T(8,128)(2,1)} %get-tuple-element.10.near_ref), channel_id=1, source_target_pairs={{0,1},{1,0},{2,3},{3,2},{4,5},{5,4},{6,7},{7,6},{8,9},{9,8},{10,11... | collective-permute-start | bytes 319496 | tf_op jit(solution)/shard_map/ppermute | solution.py:34
  119.5 2.8 %collective-permute-start.7 = (bf16[1536,512]{1,0:T(8,128)(2,1)S(1)}, bf16[1536,512]{1,0:T(8,128)(2,1)}, u32[]{:S(2)}, u32[]{:S(2)}) collective-permute-start(bf16[1536,512]{1,0:T(8,128)(2,1)S(1)} %bitcast.22), channel_id=1, source_target_pairs={{0,192},{64,0},{128,64},{192,128},{1,193},{65,1},{129,65},{193,129... | collective-permute-start | bytes 4718600 | tf_op jit(solution)/shard_map/ppermute | solution.py:39
  122.3 2.4 collective-permute-start.9
  124.8 9.9 %collective-permute-done.6.refs_1_ = bf16[1536,512]{1,0:T(8,128)(2,1)} collective-permute-done((bf16[1536,512]{1,0:T(8,128)(2,1)S(1)}, bf16[1536,512]{1,0:T(8,128)(2,1)}, u32[]{:S(2)}, u32[]{:S(2)}) %collective-permute-start.6) | collective-permute-done | bytes 1572896 | tf_op jit(solution)/shard_map/ppermute | solution.py:39
  134.7 1.9 collective-permute-start.8
  136.6 0.0 collective-permute-done.10.refs_6_
  136.6 4.6 %collective-permute-start.11 = (bf16[512,1536]{1,0:T(8,128)(2,1)}, bf16[512,1536]{1,0:T(8,128)(2,1)}, u32[]{:S(2)}, u32[]{:S(2)}) collective-permute-start(bf16[512,1536]{1,0:T(8,128)(2,1)} %collective-permute-done.10.refs_6_), channel_id=1, source_target_pairs={{0,192},{64,0},{128,64},{192,128},{1,193},{65,1},{129,65},{193,129... | collective-permute-start | bytes 4718600 | tf_op jit(solution)/shard_map/ppermute | solution.py:39
  141.2 0.0 collective-permute-done.5.far_ref
  141.2 0.6 copy-done.6
  141.8 2.6 %shard_map.130 = bf16[256,1536]{1,0:T(8,128)(2,1)} custom-call(s32[3]{0:T(128)} %pad_add_fusion.where_ref, bf16[32,1664]{1,0:T(8,128)(2,1)} %get-tuple-element.10.near_ref, bf16[32,1664]{1,0:T(8,128)(2,1)} %copy-done.6), custom_call_target="tpu_custom_call" | custom-call | tf_op jit(solution)/shard_map/pallas_call | solution.py:64
  144.5 3.9 %all-to-all-start.4 = ((bf16[32,8,1536]{2,1,0:T(8,128)(2,1)}), bf16[32,8,1536]{2,1,0:T(8,128)(2,1)S(1)}, u32[]{:S(2)}, u32[]{:S(2)}) async-start(bf16[32,8,1536]{2,1,0:T(8,128)(2,1)} %bitcast.16), calls=%async_computation.4 | async-start | bytes 1572864 | tf_op jit(solution)/shard_map/all_to_all | solution.py:25
  148.4 17.9 %collective-permute-done.7.refs_2_ = bf16[1536,512]{1,0:T(8,128)(2,1)} collective-permute-done((bf16[1536,512]{1,0:T(8,128)(2,1)S(1)}, bf16[1536,512]{1,0:T(8,128)(2,1)}, u32[]{:S(2)}, u32[]{:S(2)}) %collective-permute-start.7) | collective-permute-done | bytes 1572896 | tf_op jit(solution)/shard_map/ppermute | solution.py:39
  166.3 2.1 collective-permute-done.9.refs_5_
  168.4 33.7 %collective-permute-done.8.refs_3_ = bf16[1536,512]{1,0:T(8,128)(2,1)} collective-permute-done((bf16[1536,512]{1,0:T(8,128)(2,1)}, bf16[1536,512]{1,0:T(8,128)(2,1)}, u32[]{:S(2)}, u32[]{:S(2)}) %collective-permute-start.8) | collective-permute-done | bytes 1572896 | tf_op jit(solution)/shard_map/ppermute | solution.py:39
  202.1 0.0 collective-permute-done.11.refs_7_
  202.1 0.0 all-to-all-done.4
  202.1 0.9 copy-done
  203.0 8.4 %run_expert.1 = bf16[256,1536]{1,0:T(8,128)(2,1)} custom-call(bf16[256,1536]{1,0:T(8,128)(2,1)} %bitcast.14, bf16[1536,512]{1,0:T(8,128)(2,1)} %bitcast.20, bf16[1536,512]{1,0:T(8,128)(2,1)} %collective-permute-done.6.refs_1_, bf16[1536,512]{1,0:T(8,128)(2,1)} %collective-permute-done.7.refs_2_, bf16[1536,512]{1,0:T(8,128)(2,1)} %collective-permute-done.8.refs_3_, ...), custom_call_target="tpu_custom_call" | custom-call | tf_op jit(solution)/shard_map/run_expert/pallas_call | solution.py:333
  211.4 0.0 copy-start.12
  211.4 25.3 %all_to_all.32 = bf16[32,8,1536]{2,1,0:T(8,128)(2,1)} all-to-all(bf16[32,8,1536]{2,1,0:T(8,128)(2,1)} %bitcast.15), channel_id=1, replica_groups=mesh['yh'=2,'x'=4,'yl'=4,'z'=8,'c'=2] {'yl','z'}, dimensions={0} | all-to-all | bytes 1572864 | tf_op jit(solution)/shard_map/all_to_all | solution.py:25
  236.7 2.5 shard_map.131
  239.2 4.2 %collective-permute-start.12 = (bf16[32,1536]{1,0:T(8,128)(2,1)}, bf16[32,1536]{1,0:T(8,128)(2,1)S(1)}, u32[]{:S(2)}, u32[]{:S(2)}) collective-permute-start(bf16[32,1536]{1,0:T(8,128)(2,1)} %get-tuple-element.12), channel_id=1, source_target_pairs={{0,1},{1,0},{2,3},{3,2},{4,5},{5,4},{6,7},{7,6},{8,9},{9,8},{10,11... | collective-permute-start | bytes 294920 | tf_op jit(solution)/shard_map/ppermute | solution.py:34
  243.5 1.1 collective-permute-done.12
  244.6 1.0 convert_add_fusion
  245.6 2.1 collective-permute-start.13
  247.7 6.6 %collective-permute-done.13 = bf16[16,1536]{1,0:T(8,128)(2,1)S(1)} collective-permute-done((bf16[16,1536]{1,0:T(8,128)(2,1)S(1)}, bf16[16,1536]{1,0:T(8,128)(2,1)S(1)}, u32[]{:S(2)}, u32[]{:S(2)}) %collective-permute-start.13) | collective-permute-done | bytes 49184 | tf_op jit(solution)/shard_map/ppermute | solution.py:34
  254.4 0.6 add_convert_fusion
  (25 shorter events, 0.2 us)
Async XLA Ops:
  21.5 41.5 %copy-start.5 = (bf16[8,16,640]{2,1,0:T(8,128)(2,1)}, bf16[8,16,640]{2,1,0:T(8,128)(2,1)S(1)}, u32[]{:S(2)}) copy-start(bf16[8,16,640]{2,1,0:T(8,128)(2,1)S(1)} %all_to_all.30) | copy-start | bytes 491524
  22.3 31.1 %all-to-all-start.1 = ((bf16[8,128,256]{2,1,0:T(8,128)(2,1)}), bf16[8,128,256]{2,1,0:T(8,128)(2,1)S(1)}, u32[]{:S(2)}, u32[]{:S(2)}) async-start(bf16[8,128,256]{2,1,0:T(8,128)(2,1)} %broadcast_in_dim.2), calls=%async_computation.1 | async-start | bytes 1048576 | tf_op jit(solution)/shard_map/all_to_all | solution.py:25
  32.4 8.9 %collective-permute-start.2 = (bf16[128,384]{1,0:T(8,128)(2,1)S(1)}, bf16[128,384]{1,0:T(8,128)(2,1)S(1)}, u32[]{:S(2)}, u32[]{:S(2)}) collective-permute-start(bf16[128,384]{1,0:T(8,128)(2,1)S(1)} %slice.27), channel_id=1, source_target_pairs={{0,48},{16,0},{32,16},{48,32},{1,49},{17,1},{33,17},{49,33},{2,50}... | collective-permute-start | bytes 294920 | tf_op jit(solution)/shard_map/ppermute | solution.py:39
  34.9 8.4 %collective-permute-start.1 = (bf16[128,384]{1,0:T(8,128)(2,1)S(1)}, bf16[128,384]{1,0:T(8,128)(2,1)S(1)}, u32[]{:S(2)}, u32[]{:S(2)}) collective-permute-start(bf16[128,384]{1,0:T(8,128)(2,1)S(1)} %slice.27), channel_id=1, source_target_pairs={{0,32},{16,48},{32,0},{48,16},{1,33},{17,49},{33,1},{49,17},{2,34}... | collective-permute-start | bytes 294920 | tf_op jit(solution)/shard_map/ppermute | solution.py:39
  39.3 7.3 %collective-permute-start = (bf16[128,384]{1,0:T(8,128)(2,1)S(1)}, bf16[128,384]{1,0:T(8,128)(2,1)S(1)}, u32[]{:S(2)}, u32[]{:S(2)}) collective-permute-start(bf16[128,384]{1,0:T(8,128)(2,1)S(1)} %slice.27), channel_id=1, source_target_pairs={{0,16},{16,32},{32,48},{48,0},{1,17},{17,33},{33,49},{49,1},{2,18}... | collective-permute-start | bytes 294920 | tf_op jit(solution)/shard_map/ppermute | solution.py:39
  46.6 6.8 %copy-start.4 = (bf16[512,384]{1,0:T(8,128)(2,1)}, bf16[512,384]{1,0:T(8,128)(2,1)S(1)}, u32[]{:S(2)}) copy-start(bf16[512,384]{1,0:T(8,128)(2,1)S(1)} %pad_maximum_fusion.near_ref) | copy-start | bytes 1179652
  46.7 6.8 %collective-permute-start.3 = (bf16[512,384]{1,0:T(8,128)(2,1)S(1)}, bf16[512,384]{1,0:T(8,128)(2,1)S(1)}, u32[]{:S(2)}, u32[]{:S(2)}) collective-permute-start(bf16[512,384]{1,0:T(8,128)(2,1)S(1)} %pad_maximum_fusion.near_ref), channel_id=1, source_target_pairs={{0,1},{1,0},{2,3},{3,2},{4,5},{5,4},{6,7},{7,6},{8,9},{9,8},{10,11... | collective-permute-start | bytes 1179656 | tf_op jit(solution)/shard_map/ppermute | solution.py:34
  53.4 0.8 copy-start.7
  53.4 0.9 copy-start.1
  63.0 30.3 %copy-start.3 = (bf16[1,1536,512]{2,1,0:T(8,128)(2,1)S(1)}, bf16[1,1536,512]{2,1,0:T(8,128)(2,1)}, u32[]{:S(2)}) copy-start(bf16[1,1536,512]{2,1,0:T(8,128)(2,1)} %param.22) | copy-start | bytes 4718596
  63.0 36.9 %copy-start.13 = (f32[1536]{0:T(1024)S(1)}, f32[1536]{0:T(1024)}, u32[]{:S(2)}) copy-start(f32[1536]{0:T(1024)} %param.19) | copy-start | bytes 18436
  63.0 37.5 %copy-start.14 = (f32[1536]{0:T(1024)S(1)}, f32[1536]{0:T(1024)}, u32[]{:S(2)}) copy-start(f32[1536]{0:T(1024)} %param.20) | copy-start | bytes 18436
  86.9 14.2 %copy-start.11 = (f32[1536]{0:T(1024)S(1)}, f32[1536]{0:T(1024)}, u32[]{:S(2)}) copy-start(f32[1536]{0:T(1024)} %param.18) | copy-start | bytes 18436
  86.9 14.3 %copy-start.8 = (bf16[16,1536]{1,0:T(8,128)(2,1)S(1)}, bf16[16,1536]{1,0:T(8,128)(2,1)}, u32[]{:S(2)}) copy-start(bf16[16,1536]{1,0:T(8,128)(2,1)} %residual_ref.1) | copy-start | bytes 147460
  89.9 11.2 %all-to-all-start.3 = ((bf16[4,32,1536]{2,1,0:T(8,128)(2,1)}), bf16[4,32,1536]{2,1,0:T(8,128)(2,1)S(1)}, u32[]{:S(2)}, u32[]{:S(2)}) async-start(bf16[4,32,1536]{2,1,0:T(8,128)(2,1)} %shard_map.128), calls=%async_computation.3 | async-start | bytes 786432 | tf_op jit(solution)/shard_map/all_to_all | solution.py:25
  93.4 41.3 %collective-permute-start.6 = (bf16[1536,512]{1,0:T(8,128)(2,1)S(1)}, bf16[1536,512]{1,0:T(8,128)(2,1)}, u32[]{:S(2)}, u32[]{:S(2)}) collective-permute-start(bf16[1536,512]{1,0:T(8,128)(2,1)S(1)} %bitcast.21), channel_id=1, source_target_pairs={{0,64},{64,128},{128,192},{192,0},{1,65},{65,129},{129,193},{193,1... | collective-permute-start | bytes 4718600 | tf_op jit(solution)/shard_map/ppermute | solution.py:39
  96.7 39.9 %collective-permute-start.10 = (bf16[512,1536]{1,0:T(8,128)(2,1)}, bf16[512,1536]{1,0:T(8,128)(2,1)}, u32[]{:S(2)}, u32[]{:S(2)}) collective-permute-start(bf16[512,1536]{1,0:T(8,128)(2,1)} %bitcast.11.refs_4_), channel_id=1, source_target_pairs={{0,192},{64,0},{128,64},{192,128},{1,193},{65,1},{129,65},{193,129... | collective-permute-start | bytes 4718600 | tf_op jit(solution)/shard_map/ppermute | solution.py:39
  101.2 9.4 %copy-start.2 = (f32[32,1536]{1,0:T(8,128)}, f32[32,1536]{1,0:T(8,128)S(1)}, u32[]{:S(2)}) copy-start(f32[32,1536]{1,0:T(8,128)S(1)} %broadcast_multiply_fusion.sum_ref) | copy-start | bytes 589828
  101.3 9.4 %collective-permute-start.4 = (bf16[32,1536]{1,0:T(8,128)(2,1)S(1)}, bf16[32,1536]{1,0:T(8,128)(2,1)S(1)}, u32[]{:S(2)}, u32[]{:S(2)}) collective-permute-start(bf16[32,1536]{1,0:T(8,128)(2,1)S(1)} %pad_maximum_fusion.1), channel_id=1, source_target_pairs={{0,256},{256,0},{1,257},{257,1},{2,258},{258,2},{3,259},{259,3},{4... | collective-permute-start | bytes 294920 | tf_op jit(solution)/shard_map/ppermute | solution.py:34
  110.7 0.6 copy-start.9
  113.5 27.7 %collective-permute-start.5 = (bf16[32,1664]{1,0:T(8,128)(2,1)}, bf16[32,1664]{1,0:T(8,128)(2,1)S(1)}, u32[]{:S(2)}, u32[]{:S(2)}) collective-permute-start(bf16[32,1664]{1,0:T(8,128)(2,1)} %get-tuple-element.10.near_ref), channel_id=1, source_target_pairs={{0,1},{1,0},{2,3},{3,2},{4,5},{5,4},{6,7},{7,6},{8,9},{9,8},{10,11... | collective-permute-start | bytes 319496 | tf_op jit(solution)/shard_map/ppermute | solution.py:34
  119.5 46.8 %collective-permute-start.7 = (bf16[1536,512]{1,0:T(8,128)(2,1)S(1)}, bf16[1536,512]{1,0:T(8,128)(2,1)}, u32[]{:S(2)}, u32[]{:S(2)}) collective-permute-start(bf16[1536,512]{1,0:T(8,128)(2,1)S(1)} %bitcast.22), channel_id=1, source_target_pairs={{0,192},{64,0},{128,64},{192,128},{1,193},{65,1},{129,65},{193,129... | collective-permute-start | bytes 4718600 | tf_op jit(solution)/shard_map/ppermute | solution.py:39
  122.3 46.1 %collective-permute-start.9 = (bf16[512,1536]{1,0:T(8,128)(2,1)}, bf16[512,1536]{1,0:T(8,128)(2,1)}, u32[]{:S(2)}, u32[]{:S(2)}) collective-permute-start(bf16[512,1536]{1,0:T(8,128)(2,1)} %bitcast.11.refs_4_), channel_id=1, source_target_pairs={{0,64},{64,128},{128,192},{192,0},{1,65},{65,129},{129,193},{193,1... | collective-permute-start | bytes 4718600 | tf_op jit(solution)/shard_map/ppermute | solution.py:39
  134.7 67.4 %collective-permute-start.8 = (bf16[1536,512]{1,0:T(8,128)(2,1)}, bf16[1536,512]{1,0:T(8,128)(2,1)}, u32[]{:S(2)}, u32[]{:S(2)}) collective-permute-start(bf16[1536,512]{1,0:T(8,128)(2,1)} %collective-permute-done.6.refs_1_), channel_id=1, source_target_pairs={{0,64},{64,128},{128,192},{192,0},{1,65},{65,129},{129,193},{193,1... | collective-permute-start | bytes 4718600 | tf_op jit(solution)/shard_map/ppermute | solution.py:39
  136.6 65.5 %collective-permute-start.11 = (bf16[512,1536]{1,0:T(8,128)(2,1)}, bf16[512,1536]{1,0:T(8,128)(2,1)}, u32[]{:S(2)}, u32[]{:S(2)}) collective-permute-start(bf16[512,1536]{1,0:T(8,128)(2,1)} %collective-permute-done.10.refs_6_), channel_id=1, source_target_pairs={{0,192},{64,0},{128,64},{192,128},{1,193},{65,1},{129,65},{193,129... | collective-permute-start | bytes 4718600 | tf_op jit(solution)/shard_map/ppermute | solution.py:39
  141.2 0.6 copy-start.6
  144.5 57.6 %all-to-all-start.4 = ((bf16[32,8,1536]{2,1,0:T(8,128)(2,1)}), bf16[32,8,1536]{2,1,0:T(8,128)(2,1)S(1)}, u32[]{:S(2)}, u32[]{:S(2)}) async-start(bf16[32,8,1536]{2,1,0:T(8,128)(2,1)} %bitcast.16), calls=%async_computation.4 | async-start | bytes 1572864 | tf_op jit(solution)/shard_map/all_to_all | solution.py:25
  202.1 0.9 copy-start
  211.4 43.0 %copy-start.10 = (f32[16,1536]{1,0:T(8,128)S(1)}, f32[16,1536]{1,0:T(8,128)}, u32[]{:S(2)}) copy-start(f32[16,1536]{1,0:T(8,128)} %get-tuple-element.9) | copy-start | bytes 294916
  211.4 43.0 %copy-start.12 = (f32[1536]{0:T(1024)S(1)}, f32[1536]{0:T(1024)}, u32[]{:S(2)}) copy-start(f32[1536]{0:T(1024)} %param.21) | copy-start | bytes 18436
  239.2 5.4 %collective-permute-start.12 = (bf16[32,1536]{1,0:T(8,128)(2,1)}, bf16[32,1536]{1,0:T(8,128)(2,1)S(1)}, u32[]{:S(2)}, u32[]{:S(2)}) collective-permute-start(bf16[32,1536]{1,0:T(8,128)(2,1)} %get-tuple-element.12), channel_id=1, source_target_pairs={{0,1},{1,0},{2,3},{3,2},{4,5},{5,4},{6,7},{7,6},{8,9},{9,8},{10,11... | collective-permute-start | bytes 294920 | tf_op jit(solution)/shard_map/ppermute | solution.py:34
  245.6 8.8 %collective-permute-start.13 = (bf16[16,1536]{1,0:T(8,128)(2,1)S(1)}, bf16[16,1536]{1,0:T(8,128)(2,1)S(1)}, u32[]{:S(2)}, u32[]{:S(2)}) collective-permute-start(bf16[16,1536]{1,0:T(8,128)(2,1)S(1)} %select_convert_fusion), channel_id=1, source_target_pairs={{0,256},{256,0},{1,257},{257,1},{2,258},{258,2},{3,259},{259,3},{4... | collective-permute-start | bytes 147464 | tf_op jit(solution)/shard_map/ppermute | solution.py:34
where the time goes:
time: 257 us; the launch traced here: 255 us
  waiting for transfers between devices  84.5 us (33%)
  blocking collectives  68.9 us (27%)
  starting transfers between devices  64.5 us (25%)
  Pallas kernels  29.1 us (11%)
  local copies, waits for them, and re-layouts  5.2 us (2%)
    ppermute x9, waiting for transfers between devices, shifted(): return lax.ppermute(array, axis, [(i, (i + by) % n) for i in range(n)])  68.9 us
    all_to_all x3, blocking collectives, exchange(): return lax.all_to_all(array, axis, 0, 0, tiled=True)  68.9 us
    ppermute x9, starting transfers between devices, shifted(): return lax.ppermute(array, axis, [(i, (i + by) % n) for i in range(n)])  27.1 us
    ppermute x5, starting transfers between devices, partner(): return lax.ppermute(array, axis, [(0, 1), (1, 0)])  20 us
    all_to_all x3, starting transfers between devices, exchange(): return lax.all_to_all(array, axis, 0, 0, tiled=True)  17.4 us
    ppermute x5, waiting for transfers between devices, partner(): return lax.ppermute(array, axis, [(0, 1), (1, 0)])  15.6 us
    pallas_call x5, Pallas kernels, local(): pl.pallas_call(body, out_shape=outs, in_specs=specs, out_specs=jax.tree.m...  12.1 us
    pallas_call x1, Pallas kernels, layer(): pl.pallas_call(attend, grid=(queries.shape[0] // q_block,), in_specs=[pl....  8.64 us
  transfers between devices with their start and end apart: 17, of which 10 were waited for; matrix products, arithmetic and copies ran while one was open for 1% of the time, Pallas kernels for 2%

commit v1 on v0

--- a/solution.py
+++ b/solution.py
@@ -56,18 +56,24 @@
     return out
 
 
-def local(body, outs, *args, smem=(), **kw):
-    specs = [
-        pl.BlockSpec(memory_space=pltpu.SMEM if i in smem else pltpu.VMEM)
-        for i in range(len(args))
-    ]
+def local(body, outs, *args, smem=(), elsewhere=(), **kw):
+    specs, placed = [], []
+    for i, arg in enumerate(args):
+        if i in smem:
+            specs.append(pl.BlockSpec(memory_space=pltpu.SMEM))
+        elif i in elsewhere:
+            specs.append(pl.BlockSpec(memory_space=pl.ANY))
+        else:
+            specs.append(pl.BlockSpec(memory_space=pltpu.VMEM))
+            arg = pltpu.with_memory_space_constraint(arg, pltpu.VMEM)
+        placed.append(arg)
     return pl.pallas_call(
         body,
-        out_shape=outs,
+        out_shape=jax.tree.map(lambda o: pltpu.VMEM(o.shape, o.dtype), outs),
         in_specs=specs,
         out_specs=jax.tree.map(lambda _: pl.BlockSpec(memory_space=pltpu.VMEM), outs),
         **kw,
-    )(*args)
+    )(*placed)
 
 
 def shape(dims, kind=BF16):
@@ -95,29 +101,34 @@
 
 
 def attend(q_ref, near_ref, far_ref, out_ref):
-    rows, cols = q_ref.shape[0], q_ref.shape[1] - HD
-    heads = cols // HD
-    q = q_ref[:, :cols]
+    wide = q_ref.shape[1]
+    cols, rows = wide - HD, 256
     near_k, far_k = near_ref[:, :cols], far_ref[:, :cols]
     near_v, far_v = near_ref[:, LANES:], far_ref[:, LANES:]
     q_head = iota((rows, cols), 1) // HD
-    lane = iota((rows, cols + HD), 1)
-    out = jnp.zeros((rows, cols + HD), F32)
-    for j in range(heads):
-        q_j = jnp.where(q_head == j, q, jnp.zeros_like(q))
-        near = dot(q_j, near_k, ((1,), (1,)))
-        far = dot(q_j, far_k, ((1,), (1,)))
-        peak = jnp.maximum(
-            jnp.max(near, axis=1, keepdims=True), jnp.max(far, axis=1, keepdims=True)
-        )
-        near = jnp.exp2((near - peak) * RATE)
-        far = jnp.exp2((far - peak) * RATE)
-        total = jnp.sum(near, axis=1, keepdims=True) + jnp.sum(far, axis=1, keepdims=True)
-        accum = dot(near.astype(BF16), near_v) + dot(far.astype(BF16), far_v)
-        out = jnp.where(lane // HD == j + 1, accum * (1.0 / total), out)
-        for i, piece in enumerate(pieces(peak) + pieces(total)):
-            out = jnp.where(lane == 6 * j + i, piece, out)
-    out_ref[...] = out.astype(BF16)
+    o_head = iota((rows, wide), 1) // HD - 1
+    lane = iota((rows, LANES), 1)
+    for start in range(0, q_ref.shape[0], rows):
+        q = q_ref[start : start + rows, :cols]
+        out = jnp.zeros((rows, wide), F32)
+        stats = jnp.zeros((rows, LANES), F32)
+        for j in range(cols // HD):
+            q_j = jnp.where(q_head == j, q, jnp.zeros_like(q))
+            near = dot(q_j, near_k, ((1,), (1,)))
+            far = dot(q_j, far_k, ((1,), (1,)))
+            peak = jnp.maximum(
+                jnp.max(near, axis=1, keepdims=True), jnp.max(far, axis=1, keepdims=True)
+            )
+            near = jnp.exp2((near - peak) * RATE)
+            far = jnp.exp2((far - peak) * RATE)
+            total = jnp.sum(near, axis=1, keepdims=True) + jnp.sum(far, axis=1, keepdims=True)
+            accum = dot(near.astype(BF16), near_v) + dot(far.astype(BF16), far_v)
+            out = jnp.where(o_head == j, accum * (1.0 / total), out)
+            for i, piece in enumerate(pieces(peak) + pieces(total)):
+                stats = jnp.where(lane == 6 * j + i, piece, stats)
+        stats = jnp.where(lane < HD, stats, out[:, :LANES])
+        out_ref[start : start + rows, :LANES] = stats.astype(BF16)
+        out_ref[start : start + rows, LANES:] = out[:, LANES:].astype(BF16)
 
 
 def project(parts_ref, weight_ref, out_ref):
@@ -271,15 +282,9 @@
     factor = (1.0 + norm_scale).reshape(1, width)
     gate, shift = (a.reshape(1, width) for a in (attention_gate, norm_shift))
 
-    own = local(
-        prepare,
-        shape((n_head, tok, 3 * cols + HD)),
-        query_rows,
-        key_rows,
-        value_rows,
-        routing.T,
-        combine_weight.T,
-    )
+    own = pl.pallas_call(
+        prepare, out_shape=pltpu.VMEM((n_head, tok, 3 * cols + HD), BF16), name="prepare"
+    )(query_rows, key_rows, value_rows, routing.T, combine_weight.T)
     own = exchange(own, HEAD).reshape(rows, 3 * cols + HD)
 
     up, down = expert_up[0], expert_down[0]
@@ -291,16 +296,7 @@
     far = partner(near, "c")
     queries = gathered(own[:, : cols + HD], "z").reshape(-1, cols + HD)
 
-    q_block = 256
-    whole = pl.BlockSpec(near.shape, lambda i: (0, 0))
-    packed = pl.pallas_call(
-        attend,
-        grid=(queries.shape[0] // q_block,),
-        in_specs=[pl.BlockSpec((q_block, cols + HD), lambda i: (i, 0)), whole, whole],
-        out_specs=pl.BlockSpec((q_block, cols + HD), lambda i: (i, 0)),
-        out_shape=shape((queries.shape[0], cols + HD)),
-        name="attend",
-    )(queries, near, far)
+    packed = local(attend, shape((queries.shape[0], cols + HD)), queries, near, far)
     packed = exchange(packed.reshape(n_z, rows, cols + HD), "z")
 
     partial = local(project, shape((n_x, 2 * tok, width)), packed, out_weight)
@@ -329,19 +325,19 @@
     sent = local(dispatch, shape((buffer_rows, width)), where, near, far, smem=(0,))
     arrived = exchange(sent.reshape(n_plane, -1, width), PLANE).reshape(buffer_rows, width)
     ups, downs = (up, up_left, up_right, up_far), (down, down_left, down_right, down_far)
-    in_place = pl.BlockSpec(memory_space=pl.ANY)
-    output = pl.pallas_call(
+    output = local(
         run_expert,
-        in_specs=[pl.BlockSpec(memory_space=pltpu.VMEM)] + [in_place] * (2 * n_x),
-        out_specs=pl.BlockSpec(memory_space=pltpu.VMEM),
-        out_shape=shape((buffer_rows, width)),
+        shape((buffer_rows, width)),
+        arrived,
+        *ups,
+        *downs,
+        elsewhere=range(1, 1 + 2 * n_x),
         scratch_shapes=[
             pltpu.VMEM((n_x, *up.shape), BF16),
             pltpu.VMEM((n_x, *down.shape), BF16),
             pltpu.SemaphoreType.DMA((2, n_x)),
         ],
-        name="run_expert",
-    )(arrived, *ups, *downs)
+    )
     returned = exchange(output.reshape(n_plane, -1, width), PLANE).reshape(buffer_rows, width)
 
     kept, given = local(

time: 257 us -> 243 us (0.946)
  Pallas kernels: 29.1 us -> 19.1 us
  local copies, waits for them, and re-layouts: 5.2 us -> 0.91 us
    pallas_call x7, Pallas kernels: 29.1 us -> 19.1 us  [the longest x6 18 us: local(): pl.pallas_call(body, out_shape=jax.tree.map(lambda o: pltpu.VMEM(o.shape,...]
    unnamed x30 -> x14, local copies, waits for them, and re-layouts: 3.15 us -> 0.04 us
    ppermute x9, waiting for transfers between devices: 68.9 us -> 71.6 us  [shifted(): return lax.ppermute(array, axis, [(i, (i + by) % n) for i in range(n)])]
  transfers between devices with their start and end apart: 17 -> 17, of which waited for: 10 -> 10; matrix products, arithmetic and copies ran while one was open for 1% -> 0% of each run, Pallas kernels for 2% -> 1%
where the time goes in v1:
time: 243 us; the launch traced here: 241 us
  waiting for transfers between devices  87 us (36%)
  blocking collectives  66.5 us (27%)
  starting transfers between devices  66.1 us (27%)
  Pallas kernels  19.1 us (8%)
    ppermute x9, waiting for transfers between devices, shifted(): return lax.ppermute(array, axis, [(i, (i + by) % n) for i in range(n)])  71.6 us
    all_to_all x3, blocking collectives, exchange(): return lax.all_to_all(array, axis, 0, 0, tiled=True)  66.5 us
    ppermute x9, starting transfers between devices, shifted(): return lax.ppermute(array, axis, [(i, (i + by) % n) for i in range(n)])  27.1 us
    ppermute x5, starting transfers between devices, partner(): return lax.ppermute(array, axis, [(0, 1), (1, 0)])  21.2 us
    pallas_call x6, Pallas kernels, local(): pl.pallas_call(body, out_shape=jax.tree.map(lambda o: pltpu.VMEM(o.shape,...  18 us
    all_to_all x3, starting transfers between devices, exchange(): return lax.all_to_all(array, axis, 0, 0, tiled=True)  17.7 us
    ppermute x5, waiting for transfers between devices, partner(): return lax.ppermute(array, axis, [(0, 1), (1, 0)])  15.4 us
  transfers between devices with their start and end apart: 17, of which 10 were waited for; matrix products, arithmetic and copies ran while one was open for 0% of the time, Pallas kernels for 1%

profile of v1, /device:TPU:1, one launch (start us, length us, event | category | flops | bytes accessed | tf_op | source)
XLA Modules:
  0.0 241.4 jit_solution(10377368081296840263)
XLA Ops:
  0.0 1.1 prepare.1
  1.1 19.5 %all_to_all.30 = bf16[8,16,640]{2,1,0:T(8,128)(2,1)S(1)} all-to-all(bf16[8,16,640]{2,1,0:T(8,128)(2,1)S(1)} %prepare.1), channel_id=1, replica_groups=mesh['yh'=2,'x'=4,'yl'=4,'z'=8,'c'=2] {'yh','x'}, dimensions={0} | all-to-all | bytes 327680 | tf_op jit(solution)/shard_map/all_to_all | solution.py:25
  20.6 0.8 broadcast_in_dim.2
  21.5 10.0 %all-to-all-start.1 = ((bf16[8,128,256]{2,1,0:T(8,128)(2,1)}), bf16[8,128,256]{2,1,0:T(8,128)(2,1)S(1)}, u32[]{:S(2)}, u32[]{:S(2)}) async-start(bf16[8,128,256]{2,1,0:T(8,128)(2,1)} %broadcast_in_dim.2), calls=%async_computation.1 | async-start | bytes 1048576 | tf_op jit(solution)/shard_map/all_to_all | solution.py:25
  31.5 2.5 %collective-permute-start.2 = (bf16[128,384]{1,0:T(8,128)(2,1)S(1)}, bf16[128,384]{1,0:T(8,128)(2,1)S(1)}, u32[]{:S(2)}, u32[]{:S(2)}) collective-permute-start(bf16[128,384]{1,0:T(8,128)(2,1)S(1)} %slice.27), channel_id=1, source_target_pairs={{0,48},{16,0},{32,16},{48,32},{1,49},{17,1},{33,17},{49,33},{2,50}... | collective-permute-start | bytes 294920 | tf_op jit(solution)/shard_map/ppermute | solution.py:39
  34.1 4.4 %collective-permute-start.1 = (bf16[128,384]{1,0:T(8,128)(2,1)S(1)}, bf16[128,384]{1,0:T(8,128)(2,1)S(1)}, u32[]{:S(2)}, u32[]{:S(2)}) collective-permute-start(bf16[128,384]{1,0:T(8,128)(2,1)S(1)} %slice.27), channel_id=1, source_target_pairs={{0,32},{16,48},{32,0},{48,16},{1,33},{17,49},{33,1},{49,17},{2,34}... | collective-permute-start | bytes 294920 | tf_op jit(solution)/shard_map/ppermute | solution.py:39
  38.5 1.9 collective-permute-start
  40.4 0.0 collective-permute-done.2
  40.4 2.0 collective-permute-done.1
  42.4 3.3 %collective-permute-done = bf16[128,384]{1,0:T(8,128)(2,1)S(1)} collective-permute-done((bf16[128,384]{1,0:T(8,128)(2,1)S(1)}, bf16[128,384]{1,0:T(8,128)(2,1)S(1)}, u32[]{:S(2)}, u32[]{:S(2)}) %collective-permute-start) | collective-permute-done | bytes 98336 | tf_op jit(solution)/shard_map/ppermute | solution.py:39
  45.8 0.0 copy-start
  45.8 5.6 %collective-permute-start.3 = (bf16[512,384]{1,0:T(8,128)(2,1)S(1)}, bf16[512,384]{1,0:T(8,128)(2,1)S(1)}, u32[]{:S(2)}, u32[]{:S(2)}) collective-permute-start(bf16[512,384]{1,0:T(8,128)(2,1)S(1)} %pad_maximum_fusion.near_ref), channel_id=1, source_target_pairs={{0,1},{1,0},{2,3},{3,2},{4,5},{5,4},{6,7},{7,6},{8,9},{9,8},{10,11... | collective-permute-start | bytes 1179656 | tf_op jit(solution)/shard_map/ppermute | solution.py:34
  51.4 1.3 collective-permute-done.3.far_ref
  52.7 0.0 all-to-all-done.1
  52.7 5.3 %shard_map.127 = bf16[1024,256]{1,0:T(8,128)(2,1)S(1)} custom-call(bf16[1024,256]{1,0:T(8,128)(2,1)S(1)} %bitcast.17, bf16[512,384]{1,0:T(8,128)(2,1)S(1)} %pad_maximum_fusion.near_ref, bf16[512,384]{1,0:T(8,128)(2,1)S(1)} %collective-permute-done.3.far_ref), custom_call_target="tpu_custom_call" | custom-call | tf_op jit(solution)/shard_map/pallas_call | solution.py:70
  58.1 0.0 copy-start.5
  58.1 0.0 copy-start.6
  58.1 23.4 %all_to_all.31.parts_ref = bf16[8,128,256]{2,1,0:T(8,128)(2,1)S(1)} all-to-all(bf16[8,128,256]{2,1,0:T(8,128)(2,1)S(1)} %bitcast.18), channel_id=1, replica_groups=mesh['yh'=2,'x'=4,'yl'=4,'z'=8,'c'=2] {'z'}, dimensions={0} | all-to-all | bytes 1048576 | tf_op jit(solution)/shard_map/all_to_all | solution.py:25
  81.5 0.0 copy-done
  81.5 0.0 copy-start.3
  81.5 0.0 copy-start.1
  81.5 1.7 shard_map.128
  83.2 0.0 copy-start.2
  83.2 3.6 %all-to-all-start.3 = ((bf16[4,32,1536]{2,1,0:T(8,128)(2,1)}), bf16[4,32,1536]{2,1,0:T(8,128)(2,1)S(1)}, u32[]{:S(2)}, u32[]{:S(2)}) async-start(bf16[4,32,1536]{2,1,0:T(8,128)(2,1)} %shard_map.128), calls=%async_computation.3 | async-start | bytes 786432 | tf_op jit(solution)/shard_map/all_to_all | solution.py:25
  86.8 3.3 %collective-permute-start.6 = (bf16[1536,512]{1,0:T(8,128)(2,1)}, bf16[1536,512]{1,0:T(8,128)(2,1)}, u32[]{:S(2)}, u32[]{:S(2)}) collective-permute-start(bf16[1536,512]{1,0:T(8,128)(2,1)} %bitcast.22), channel_id=1, source_target_pairs={{0,64},{64,128},{128,192},{192,0},{1,65},{65,129},{129,193},{193,1... | collective-permute-start | bytes 4718600 | tf_op jit(solution)/shard_map/ppermute | solution.py:39
  90.2 3.2 %collective-permute-start.10 = (bf16[512,1536]{1,0:T(8,128)(2,1)}, bf16[512,1536]{1,0:T(8,128)(2,1)}, u32[]{:S(2)}, u32[]{:S(2)}) collective-permute-start(bf16[512,1536]{1,0:T(8,128)(2,1)} %bitcast.11.refs_4_), channel_id=1, source_target_pairs={{0,192},{64,0},{128,64},{192,128},{1,193},{65,1},{129,65},{193,129... | collective-permute-start | bytes 4718600 | tf_op jit(solution)/shard_map/ppermute | solution.py:39
  93.4 0.0 copy-done.5
  93.4 0.0 copy-done.6
  93.4 0.0 all-to-all-done.3
  93.4 0.1 convert_reduce_fusion
  93.5 0.0 copy-done.3
  93.5 0.0 copy-done.1
  93.6 2.2 collective-permute-start.4
  95.8 0.6 pad_add_fusion.where_ref
  96.4 6.5 %collective-permute-done.4.got_ref = bf16[32,1536]{1,0:T(8,128)(2,1)S(1)} collective-permute-done((bf16[32,1536]{1,0:T(8,128)(2,1)S(1)}, bf16[32,1536]{1,0:T(8,128)(2,1)S(1)}, u32[]{:S(2)}, u32[]{:S(2)}) %collective-permute-start.4) | collective-permute-done | bytes 98336 | tf_op jit(solution)/shard_map/ppermute | solution.py:34
  102.9 1.1 shard_map.129
  104.0 7.1 %collective-permute-start.5 = (bf16[32,1664]{1,0:T(8,128)(2,1)S(1)}, bf16[32,1664]{1,0:T(8,128)(2,1)S(1)}, u32[]{:S(2)}, u32[]{:S(2)}) collective-permute-start(bf16[32,1664]{1,0:T(8,128)(2,1)S(1)} %get-tuple-element.10.near_ref), channel_id=1, source_target_pairs={{0,1},{1,0},{2,3},{3,2},{4,5},{5,4},{6,7},{7,6},{8,9},{9,8},{10,11... | collective-permute-start | bytes 319496 | tf_op jit(solution)/shard_map/ppermute | solution.py:34
  111.0 0.0 copy-done.2
  111.0 1.9 collective-permute-start.7
  113.0 3.4 %collective-permute-start.9 = (bf16[512,1536]{1,0:T(8,128)(2,1)}, bf16[512,1536]{1,0:T(8,128)(2,1)}, u32[]{:S(2)}, u32[]{:S(2)}) collective-permute-start(bf16[512,1536]{1,0:T(8,128)(2,1)} %bitcast.11.refs_4_), channel_id=1, source_target_pairs={{0,64},{64,128},{128,192},{192,0},{1,65},{65,129},{129,193},{193,1... | collective-permute-start | bytes 4718600 | tf_op jit(solution)/shard_map/ppermute | solution.py:39
  116.3 11.8 %collective-permute-done.6.refs_1_ = bf16[1536,512]{1,0:T(8,128)(2,1)} collective-permute-done((bf16[1536,512]{1,0:T(8,128)(2,1)}, bf16[1536,512]{1,0:T(8,128)(2,1)}, u32[]{:S(2)}, u32[]{:S(2)}) %collective-permute-start.6) | collective-permute-done | bytes 1572896 | tf_op jit(solution)/shard_map/ppermute | solution.py:39
  128.2 1.9 collective-permute-start.8
  130.1 0.0 collective-permute-done.10.refs_6_
  130.1 4.6 %collective-permute-start.11 = (bf16[512,1536]{1,0:T(8,128)(2,1)}, bf16[512,1536]{1,0:T(8,128)(2,1)}, u32[]{:S(2)}, u32[]{:S(2)}) collective-permute-start(bf16[512,1536]{1,0:T(8,128)(2,1)} %collective-permute-done.10.refs_6_), channel_id=1, source_target_pairs={{0,192},{64,0},{128,64},{192,128},{1,193},{65,1},{129,65},{193,129... | collective-permute-start | bytes 4718600 | tf_op jit(solution)/shard_map/ppermute | solution.py:39
  134.7 0.0 collective-permute-done.5.far_ref
  134.7 2.3 shard_map.130
  137.0 4.1 %all-to-all-start.4 = ((bf16[32,8,1536]{2,1,0:T(8,128)(2,1)}), bf16[32,8,1536]{2,1,0:T(8,128)(2,1)S(1)}, u32[]{:S(2)}, u32[]{:S(2)}) async-start(bf16[32,8,1536]{2,1,0:T(8,128)(2,1)} %bitcast.8), calls=%async_computation.4 | async-start | bytes 1572864 | tf_op jit(solution)/shard_map/all_to_all | solution.py:25
  141.1 18.6 %collective-permute-done.7.refs_2_ = bf16[1536,512]{1,0:T(8,128)(2,1)} collective-permute-done((bf16[1536,512]{1,0:T(8,128)(2,1)S(1)}, bf16[1536,512]{1,0:T(8,128)(2,1)}, u32[]{:S(2)}, u32[]{:S(2)}) %collective-permute-start.7) | collective-permute-done | bytes 1572896 | tf_op jit(solution)/shard_map/ppermute | solution.py:39
  159.7 2.1 collective-permute-done.9.refs_5_
  161.9 33.7 %collective-permute-done.8.refs_3_ = bf16[1536,512]{1,0:T(8,128)(2,1)} collective-permute-done((bf16[1536,512]{1,0:T(8,128)(2,1)}, bf16[1536,512]{1,0:T(8,128)(2,1)}, u32[]{:S(2)}, u32[]{:S(2)}) %collective-permute-start.8) | collective-permute-done | bytes 1572896 | tf_op jit(solution)/shard_map/ppermute | solution.py:39
  195.6 0.0 collective-permute-done.11.refs_7_
  195.6 0.0 all-to-all-done.4
  195.6 6.3 %shard_map.131 = bf16[256,1536]{1,0:T(8,128)(2,1)S(1)} custom-call(bf16[256,1536]{1,0:T(8,128)(2,1)S(1)} %bitcast.14, bf16[1536,512]{1,0:T(8,128)(2,1)} %bitcast.23, bf16[1536,512]{1,0:T(8,128)(2,1)} %collective-permute-done.6.refs_1_, bf16[1536,512]{1,0:T(8,128)(2,1)} %collective-permute-done.7.refs_2_, bf16[1536,512]{1,0:T(8,128)(2,1)} %collective-permute-done.8.refs_3_, ...), custom_call_target="tpu_custom_call" | custom-call | tf_op jit(solution)/shard_map/pallas_call | solution.py:70
  201.9 0.0 copy-start.4
  202.0 23.6 %all_to_all.32 = bf16[32,8,1536]{2,1,0:T(8,128)(2,1)S(1)} all-to-all(bf16[32,8,1536]{2,1,0:T(8,128)(2,1)S(1)} %bitcast.15), channel_id=1, replica_groups=mesh['yh'=2,'x'=4,'yl'=4,'z'=8,'c'=2] {'yl','z'}, dimensions={0} | all-to-all | bytes 1572864 | tf_op jit(solution)/shard_map/all_to_all | solution.py:25
  225.5 1.2 shard_map.132
  226.8 4.2 %collective-permute-start.12 = (bf16[32,1536]{1,0:T(8,128)(2,1)S(1)}, bf16[32,1536]{1,0:T(8,128)(2,1)S(1)}, u32[]{:S(2)}, u32[]{:S(2)}) collective-permute-start(bf16[32,1536]{1,0:T(8,128)(2,1)S(1)} %get-tuple-element.12), channel_id=1, source_target_pairs={{0,1},{1,0},{2,3},{3,2},{4,5},{5,4},{6,7},{7,6},{8,9},{9,8},{10,11... | collective-permute-start | bytes 294920 | tf_op jit(solution)/shard_map/ppermute | solution.py:34
  231.0 0.9 collective-permute-done.12
  232.0 2.2 collective-permute-start.13
  234.1 6.6 %collective-permute-done.13 = bf16[16,1536]{1,0:T(8,128)(2,1)S(1)} collective-permute-done((bf16[16,1536]{1,0:T(8,128)(2,1)S(1)}, bf16[16,1536]{1,0:T(8,128)(2,1)S(1)}, u32[]{:S(2)}, u32[]{:S(2)}) %collective-permute-start.13) | collective-permute-done | bytes 49184 | tf_op jit(solution)/shard_map/ppermute | solution.py:34
  240.7 0.0 copy-done.4
  240.8 0.7 add_convert_fusion
  (11 shorter events, 0.2 us)
Async XLA Ops:
  21.5 31.2 %all-to-all-start.1 = ((bf16[8,128,256]{2,1,0:T(8,128)(2,1)}), bf16[8,128,256]{2,1,0:T(8,128)(2,1)S(1)}, u32[]{:S(2)}, u32[]{:S(2)}) async-start(bf16[8,128,256]{2,1,0:T(8,128)(2,1)} %broadcast_in_dim.2), calls=%async_computation.1 | async-start | bytes 1048576 | tf_op jit(solution)/shard_map/all_to_all | solution.py:25
  31.5 8.9 %collective-permute-start.2 = (bf16[128,384]{1,0:T(8,128)(2,1)S(1)}, bf16[128,384]{1,0:T(8,128)(2,1)S(1)}, u32[]{:S(2)}, u32[]{:S(2)}) collective-permute-start(bf16[128,384]{1,0:T(8,128)(2,1)S(1)} %slice.27), channel_id=1, source_target_pairs={{0,48},{16,0},{32,16},{48,32},{1,49},{17,1},{33,17},{49,33},{2,50}... | collective-permute-start | bytes 294920 | tf_op jit(solution)/shard_map/ppermute | solution.py:39
  34.1 8.4 %collective-permute-start.1 = (bf16[128,384]{1,0:T(8,128)(2,1)S(1)}, bf16[128,384]{1,0:T(8,128)(2,1)S(1)}, u32[]{:S(2)}, u32[]{:S(2)}) collective-permute-start(bf16[128,384]{1,0:T(8,128)(2,1)S(1)} %slice.27), channel_id=1, source_target_pairs={{0,32},{16,48},{32,0},{48,16},{1,33},{17,49},{33,1},{49,17},{2,34}... | collective-permute-start | bytes 294920 | tf_op jit(solution)/shard_map/ppermute | solution.py:39
  38.5 7.3 %collective-permute-start = (bf16[128,384]{1,0:T(8,128)(2,1)S(1)}, bf16[128,384]{1,0:T(8,128)(2,1)S(1)}, u32[]{:S(2)}, u32[]{:S(2)}) collective-permute-start(bf16[128,384]{1,0:T(8,128)(2,1)S(1)} %slice.27), channel_id=1, source_target_pairs={{0,16},{16,32},{32,48},{48,0},{1,17},{17,33},{33,49},{49,1},{2,18}... | collective-permute-start | bytes 294920 | tf_op jit(solution)/shard_map/ppermute | solution.py:39
  45.8 35.7 %copy-start = (bf16[192,1536]{1,0:T(8,128)(2,1)S(1)}, bf16[192,1536]{1,0:T(8,128)(2,1)}, u32[]{:S(2)}) copy-start(bf16[192,1536]{1,0:T(8,128)(2,1)} %weight_ref.1) | copy-start | bytes 1769476
  45.8 6.9 %collective-permute-start.3 = (bf16[512,384]{1,0:T(8,128)(2,1)S(1)}, bf16[512,384]{1,0:T(8,128)(2,1)S(1)}, u32[]{:S(2)}, u32[]{:S(2)}) collective-permute-start(bf16[512,384]{1,0:T(8,128)(2,1)S(1)} %pad_maximum_fusion.near_ref), channel_id=1, source_target_pairs={{0,1},{1,0},{2,3},{3,2},{4,5},{5,4},{6,7},{7,6},{8,9},{9,8},{10,11... | collective-permute-start | bytes 1179656 | tf_op jit(solution)/shard_map/ppermute | solution.py:34
  58.1 35.3 %copy-start.5 = (f32[1536]{0:T(1024)S(1)}, f32[1536]{0:T(1024)}, u32[]{:S(2)}) copy-start(f32[1536]{0:T(1024)} %param.19) | copy-start | bytes 18436
  58.1 35.3 %copy-start.6 = (f32[1536]{0:T(1024)S(1)}, f32[1536]{0:T(1024)}, u32[]{:S(2)}) copy-start(f32[1536]{0:T(1024)} %param.20) | copy-start | bytes 18436
  81.5 12.0 %copy-start.3 = (f32[1536]{0:T(1024)S(1)}, f32[1536]{0:T(1024)}, u32[]{:S(2)}) copy-start(f32[1536]{0:T(1024)} %param.18) | copy-start | bytes 18436
  81.5 12.0 %copy-start.1 = (bf16[16,1536]{1,0:T(8,128)(2,1)S(1)}, bf16[16,1536]{1,0:T(8,128)(2,1)}, u32[]{:S(2)}) copy-start(bf16[16,1536]{1,0:T(8,128)(2,1)} %residual_ref.1) | copy-start | bytes 147460
  83.2 27.8 %copy-start.2 = (bf16[1,1536,512]{2,1,0:T(8,128)(2,1)S(1)}, bf16[1,1536,512]{2,1,0:T(8,128)(2,1)}, u32[]{:S(2)}) copy-start(bf16[1,1536,512]{2,1,0:T(8,128)(2,1)} %param.22) | copy-start | bytes 4718596
  83.2 10.2 %all-to-all-start.3 = ((bf16[4,32,1536]{2,1,0:T(8,128)(2,1)}), bf16[4,32,1536]{2,1,0:T(8,128)(2,1)S(1)}, u32[]{:S(2)}, u32[]{:S(2)}) async-start(bf16[4,32,1536]{2,1,0:T(8,128)(2,1)} %shard_map.128), calls=%async_computation.3 | async-start | bytes 786432 | tf_op jit(solution)/shard_map/all_to_all | solution.py:25
  86.8 41.3 %collective-permute-start.6 = (bf16[1536,512]{1,0:T(8,128)(2,1)}, bf16[1536,512]{1,0:T(8,128)(2,1)}, u32[]{:S(2)}, u32[]{:S(2)}) collective-permute-start(bf16[1536,512]{1,0:T(8,128)(2,1)} %bitcast.22), channel_id=1, source_target_pairs={{0,64},{64,128},{128,192},{192,0},{1,65},{65,129},{129,193},{193,1... | collective-permute-start | bytes 4718600 | tf_op jit(solution)/shard_map/ppermute | solution.py:39
  90.2 39.9 %collective-permute-start.10 = (bf16[512,1536]{1,0:T(8,128)(2,1)}, bf16[512,1536]{1,0:T(8,128)(2,1)}, u32[]{:S(2)}, u32[]{:S(2)}) collective-permute-start(bf16[512,1536]{1,0:T(8,128)(2,1)} %bitcast.11.refs_4_), channel_id=1, source_target_pairs={{0,192},{64,0},{128,64},{192,128},{1,193},{65,1},{129,65},{193,129... | collective-permute-start | bytes 4718600 | tf_op jit(solution)/shard_map/ppermute | solution.py:39
  93.6 9.3 %collective-permute-start.4 = (bf16[32,1536]{1,0:T(8,128)(2,1)S(1)}, bf16[32,1536]{1,0:T(8,128)(2,1)S(1)}, u32[]{:S(2)}, u32[]{:S(2)}) collective-permute-start(bf16[32,1536]{1,0:T(8,128)(2,1)S(1)} %pad_maximum_fusion.1), channel_id=1, source_target_pairs={{0,256},{256,0},{1,257},{257,1},{2,258},{258,2},{3,259},{259,3},{4... | collective-permute-start | bytes 294920 | tf_op jit(solution)/shard_map/ppermute | solution.py:34
  104.0 30.7 %collective-permute-start.5 = (bf16[32,1664]{1,0:T(8,128)(2,1)S(1)}, bf16[32,1664]{1,0:T(8,128)(2,1)S(1)}, u32[]{:S(2)}, u32[]{:S(2)}) collective-permute-start(bf16[32,1664]{1,0:T(8,128)(2,1)S(1)} %get-tuple-element.10.near_ref), channel_id=1, source_target_pairs={{0,1},{1,0},{2,3},{3,2},{4,5},{5,4},{6,7},{7,6},{8,9},{9,8},{10,11... | collective-permute-start | bytes 319496 | tf_op jit(solution)/shard_map/ppermute | solution.py:34
  111.0 48.7 %collective-permute-start.7 = (bf16[1536,512]{1,0:T(8,128)(2,1)S(1)}, bf16[1536,512]{1,0:T(8,128)(2,1)}, u32[]{:S(2)}, u32[]{:S(2)}) collective-permute-start(bf16[1536,512]{1,0:T(8,128)(2,1)S(1)} %bitcast.24), channel_id=1, source_target_pairs={{0,192},{64,0},{128,64},{192,128},{1,193},{65,1},{129,65},{193,129... | collective-permute-start | bytes 4718600 | tf_op jit(solution)/shard_map/ppermute | solution.py:39
  113.0 48.9 %collective-permute-start.9 = (bf16[512,1536]{1,0:T(8,128)(2,1)}, bf16[512,1536]{1,0:T(8,128)(2,1)}, u32[]{:S(2)}, u32[]{:S(2)}) collective-permute-start(bf16[512,1536]{1,0:T(8,128)(2,1)} %bitcast.11.refs_4_), channel_id=1, source_target_pairs={{0,64},{64,128},{128,192},{192,0},{1,65},{65,129},{129,193},{193,1... | collective-permute-start | bytes 4718600 | tf_op jit(solution)/shard_map/ppermute | solution.py:39
  128.2 67.4 %collective-permute-start.8 = (bf16[1536,512]{1,0:T(8,128)(2,1)}, bf16[1536,512]{1,0:T(8,128)(2,1)}, u32[]{:S(2)}, u32[]{:S(2)}) collective-permute-start(bf16[1536,512]{1,0:T(8,128)(2,1)} %collective-permute-done.6.refs_1_), channel_id=1, source_target_pairs={{0,64},{64,128},{128,192},{192,0},{1,65},{65,129},{129,193},{193,1... | collective-permute-start | bytes 4718600 | tf_op jit(solution)/shard_map/ppermute | solution.py:39
  130.1 65.5 %collective-permute-start.11 = (bf16[512,1536]{1,0:T(8,128)(2,1)}, bf16[512,1536]{1,0:T(8,128)(2,1)}, u32[]{:S(2)}, u32[]{:S(2)}) collective-permute-start(bf16[512,1536]{1,0:T(8,128)(2,1)} %collective-permute-done.10.refs_6_), channel_id=1, source_target_pairs={{0,192},{64,0},{128,64},{192,128},{1,193},{65,1},{129,65},{193,129... | collective-permute-start | bytes 4718600 | tf_op jit(solution)/shard_map/ppermute | solution.py:39
  137.0 58.6 %all-to-all-start.4 = ((bf16[32,8,1536]{2,1,0:T(8,128)(2,1)}), bf16[32,8,1536]{2,1,0:T(8,128)(2,1)S(1)}, u32[]{:S(2)}, u32[]{:S(2)}) async-start(bf16[32,8,1536]{2,1,0:T(8,128)(2,1)} %bitcast.8), calls=%async_computation.4 | async-start | bytes 1572864 | tf_op jit(solution)/shard_map/all_to_all | solution.py:25
  201.9 38.8 %copy-start.4 = (f32[1536]{0:T(1024)S(1)}, f32[1536]{0:T(1024)}, u32[]{:S(2)}) copy-start(f32[1536]{0:T(1024)} %param.21) | copy-start | bytes 18436
  226.8 5.2 %collective-permute-start.12 = (bf16[32,1536]{1,0:T(8,128)(2,1)S(1)}, bf16[32,1536]{1,0:T(8,128)(2,1)S(1)}, u32[]{:S(2)}, u32[]{:S(2)}) collective-permute-start(bf16[32,1536]{1,0:T(8,128)(2,1)S(1)} %get-tuple-element.12), channel_id=1, source_target_pairs={{0,1},{1,0},{2,3},{3,2},{4,5},{5,4},{6,7},{7,6},{8,9},{9,8},{10,11... | collective-permute-start | bytes 294920 | tf_op jit(solution)/shard_map/ppermute | solution.py:34
  232.0 8.8 %collective-permute-start.13 = (bf16[16,1536]{1,0:T(8,128)(2,1)S(1)}, bf16[16,1536]{1,0:T(8,128)(2,1)S(1)}, u32[]{:S(2)}, u32[]{:S(2)}) collective-permute-start(bf16[16,1536]{1,0:T(8,128)(2,1)S(1)} %select_convert_fusion), channel_id=1, source_target_pairs={{0,256},{256,0},{1,257},{257,1},{2,258},{258,2},{3,259},{259,3},{4... | collective-permute-start | bytes 147464 | tf_op jit(solution)/shard_map/ppermute | solution.py:34
